TPU v7x, 32 devices: a whole 2x2x4 slice. The times are simulated.
32 devices in a mesh: row: 16 (over z, x, core), col: 2 (over y).
Axes of the slice: x: 2, y: 2, z: 4, core: 2. Of those that a mesh axis runs over, the one named last changes fastest.
Arguments:
- qkv: bfloat16 [256, 16, 3, 3072], P('row', 'col'), may hold values from -6 to 6
- cotangent: bfloat16 [256, 16, 3072], P('row', 'col'), may hold values from -6 to 6
- norm_gains: float32 [2, 128], replicated, may hold values from 0.1 to 1.9
- rel_table: float32 [24, 15, 15], replicated, may hold values from -6 to 250
- shifts: int32 [2], replicated, may hold values from 1 to 7
- mask_ids: int32 [256, 16], replicated, may hold values from 0 to 2
Outputs:
- attention: bfloat16 [256, 16, 3072], P('row', 'col')
- d_qkv: bfloat16 [256, 16, 3, 3072], P('row', 'col')
- d_gains: float32 [2, 128], replicated
- d_table: float32 [24, 15, 15], replicated
All inputs are finite; a program needn't handle non-finite values.
Results may differ from a plain program's by a relative error of at most 0.0073.
Values may be sent and summed in bfloat16 or wider, within the bound.
A program may use at most 192 MiB of HBM per device.

v0:
```python
import math
import jax
import jax.numpy as jnp
from jax import lax
from jax.sharding import PartitionSpec as P

EPSILON = 1e-06
NEG_FILL = -1e30


def shifted(value, axis, steps):
    count = lax.axis_size(axis)
    pairs = [(source, (source + steps) % count) for source in range(count)]
    return lax.ppermute(value, axis, pairs)


def head_norm(inputs, gain_vec):
    values = inputs.astype(jnp.float32)
    average = jnp.mean(values, axis=-1, keepdims=True)
    centred = values - average
    variance = jnp.mean(centred * centred, axis=-1, keepdims=True)
    inv_sigma = lax.rsqrt(variance + EPSILON)
    x_hat = centred * inv_sigma
    return (x_hat, inv_sigma, (x_hat * gain_vec).astype(jnp.bfloat16))


def norm_back(x_hat, inv_sigma, d_normed, gain_vec):
    d_hat = d_normed * gain_vec
    first_mean = jnp.mean(d_hat, axis=-1, keepdims=True)
    second_mean = jnp.mean(d_hat * x_hat, axis=-1, keepdims=True)
    d_input = inv_sigma * (d_hat - first_mean - x_hat * second_mean)
    d_gain = jnp.sum(d_normed * x_hat, axis=tuple(range(d_normed.ndim - 1)))
    return (d_input, d_gain)


def offset_table(window_size):
    span_count = 2 * window_size - 1
    places = jnp.arange(window_size * window_size, dtype=jnp.int32)
    row_pos = places // window_size
    col_pos = places % window_size
    code_grid = (row_pos[:, None] - row_pos[None, :] + window_size - 1) * span_count + (
        col_pos[:, None] - col_pos[None, :] + window_size - 1
    )
    codes = jnp.arange(span_count * span_count, dtype=jnp.int32)
    return (code_grid[:, :, None] == codes[None, None, :]).astype(jnp.float32)


def to_windows(field, window_size):
    row_count, col_count = (field.shape[0], field.shape[1])
    trailing = field.shape[2:]
    blocks = field.reshape(
        (row_count // window_size, window_size, col_count // window_size, window_size) + trailing
    )
    blocks = jnp.moveaxis(blocks, 2, 1)
    return blocks.reshape(
        (row_count // window_size * (col_count // window_size), window_size * window_size)
        + trailing
    )


def from_windows(blocks, window_size, row_count, col_count):
    trailing = blocks.shape[2:]
    field = blocks.reshape(
        (row_count // window_size, col_count // window_size, window_size, window_size) + trailing
    )
    field = jnp.moveaxis(field, 1, 2)
    return field.reshape((row_count, col_count) + trailing)


def window_core(q_norm, k_norm, values, grads, pos_bias, allowed, score_scale):
    scores = (
        jnp.einsum("wqhd,wkhd->whqk", q_norm, k_norm, preferred_element_type=jnp.float32)
        * score_scale
        + pos_bias[None]
    )
    scores = jnp.where(allowed[:, None], scores, NEG_FILL)
    row_max = jnp.max(scores, axis=-1, keepdims=True)
    weights = jnp.exp(scores - row_max)
    probs = weights / jnp.sum(weights, axis=-1, keepdims=True)
    probs_b = probs.astype(jnp.bfloat16)
    output = jnp.einsum("whqk,wkhd->wqhd", probs_b, values, preferred_element_type=jnp.float32)
    d_probs = jnp.einsum("wqhd,wkhd->whqk", grads, values, preferred_element_type=jnp.float32)
    row_dot = jnp.sum(probs * d_probs, axis=-1, keepdims=True)
    d_scores = probs * (d_probs - row_dot)
    d_scores_b = d_scores.astype(jnp.bfloat16)
    d_qnorm = (
        jnp.einsum("whqk,wkhd->wqhd", d_scores_b, k_norm, preferred_element_type=jnp.float32)
        * score_scale
    )
    d_knorm = (
        jnp.einsum("whqk,wqhd->wkhd", d_scores_b, q_norm, preferred_element_type=jnp.float32)
        * score_scale
    )
    d_value = jnp.einsum("whqk,wqhd->wkhd", probs_b, grads, preferred_element_type=jnp.float32)
    return (output, d_qnorm, d_knorm, d_value, jnp.sum(d_scores, axis=0))


def label_pairs(labels, window_size):
    label_win = to_windows(labels, window_size)
    return label_win[:, :, None] == label_win[:, None, :]


def local(qkv, cotangent, norm_gains, rel_table, shifts, mask_ids):
    tile_rows, tile_cols = (qkv.shape[0], qkv.shape[1])
    feature_width = qkv.shape[3]
    head_count = rel_table.shape[0]
    head_dim = feature_width // head_count
    span_count = rel_table.shape[1]
    window_size = (span_count + 1) // 2
    score_scale = 1.0 / math.sqrt(head_dim)
    shift_row = shifts[0]
    shift_col = shifts[1]
    grid_row = lax.axis_index("row") * tile_rows
    grid_col = lax.axis_index("col") * tile_cols
    one_hot = offset_table(window_size)
    pos_bias = jnp.einsum(
        "hc,qkc->hqk",
        rel_table.reshape(head_count, span_count * span_count),
        one_hot,
        precision=lax.Precision.HIGHEST,
    )
    gain_q = norm_gains[0]
    gain_k = norm_gains[1]
    stacked = jnp.concatenate([qkv, cotangent[:, :, None]], axis=2)
    received = shifted(stacked[:window_size], "row", -1)
    rolled = lax.dynamic_slice_in_dim(
        jnp.concatenate([stacked, received], axis=0), shift_row, tile_rows, 0
    )
    received = shifted(rolled, "col", -1)
    rolled = lax.dynamic_slice_in_dim(
        jnp.concatenate([rolled, received], axis=1), shift_col, tile_cols, 1
    )
    fields = rolled.reshape(tile_rows, tile_cols, 4, head_count, head_dim)
    q_hat, q_inv, q_norm = head_norm(fields[:, :, 0], gain_q)
    k_hat, k_inv, k_norm = head_norm(fields[:, :, 1], gain_k)
    labels = jnp.roll(mask_ids, (-(grid_row + shift_row), -(grid_col + shift_col)), (0, 1))[
        :tile_rows, :tile_cols
    ]
    output, d_qnorm, d_knorm, d_value, d_bias = window_core(
        to_windows(q_norm, window_size),
        to_windows(k_norm, window_size),
        to_windows(fields[:, :, 2], window_size),
        to_windows(fields[:, :, 3], window_size),
        pos_bias,
        label_pairs(labels, window_size),
        score_scale,
    )
    output = from_windows(output, window_size, tile_rows, tile_cols)
    d_qnorm = from_windows(d_qnorm, window_size, tile_rows, tile_cols)
    d_knorm = from_windows(d_knorm, window_size, tile_rows, tile_cols)
    d_value = from_windows(d_value, window_size, tile_rows, tile_cols)
    d_query, dgain_q = norm_back(q_hat, q_inv, d_qnorm, gain_q)
    d_key, dgain_k = norm_back(k_hat, k_inv, d_knorm, gain_k)
    results = (
        jnp.stack([output, d_query, d_key, d_value], axis=2)
        .reshape(tile_rows, tile_cols, 4, feature_width)
        .astype(jnp.bfloat16)
    )
    received = shifted(results[tile_rows - window_size :], "row", 1)
    results = lax.dynamic_slice_in_dim(
        jnp.concatenate([received, results], axis=0), window_size - shift_row, tile_rows, 0
    )
    received = shifted(results, "col", 1)
    results = lax.dynamic_slice_in_dim(
        jnp.concatenate([received, results], axis=1), window_size - shift_col, tile_cols, 1
    )
    attention = results[:, :, 0]
    d_qkv = results[:, :, 1:]
    table_local = jnp.einsum("hqk,qkc->hc", d_bias, one_hot, precision=lax.Precision.HIGHEST)
    totals = lax.psum((jnp.stack([dgain_q, dgain_k]), table_local), ("row", "col"))
    return (attention, d_qkv, totals[0], totals[1].reshape(head_count, span_count, span_count))


def solution(mesh):
    placed = (P("row", "col", None, None), P("row", "col", None), P(), P(), P(), P())
    return jax.shard_map(
        local,
        mesh=mesh,
        in_specs=placed,
        out_specs=(P("row", "col", None), P("row", "col", None, None), P(), P()),
        check_vma=False,
    )
```

profile of v0, /device:TPU:0, one launch (start us, length us, event | category | flops | bytes accessed | tf_op | source)
XLA Modules:
  0.0 298.4 jit_solution(15147776239652918049)
XLA Ops:
  0.6 1.5 pad_maximum_fusion
  2.2 5.5 %collective-permute-start = (bf16[8,8,4,3072]{3,1,2,0:T(8,128)(2,1)S(1)}, bf16[8,8,4,3072]{3,1,2,0:T(8,128)(2,1)}, u32[]{:S(2)}, u32[]{:S(2)}) collective-permute-start(bf16[8,8,4,3072]{3,1,2,0:T(8,128)(2,1)S(1)} %pad_maximum_fusion), channel_id=1, source_target_pairs={{0,30},{2,0},{4,2},{6,4},{8,6},{10,8},{12,10},{14,12},{16,14},{18,... | collective-permute-start | bytes 4718600 | tf_op jit(solution)/shard_map/ppermute | solution.py:14
  10.2 15.4 %collective-permute-done = bf16[8,8,4,3072]{3,1,2,0:T(8,128)(2,1)} collective-permute-done((bf16[8,8,4,3072]{3,1,2,0:T(8,128)(2,1)S(1)}, bf16[8,8,4,3072]{3,1,2,0:T(8,128)(2,1)}, u32[]{:S(2)}, u32[]{:S(2)}) %collective-permute-start) | collective-permute-done | bytes 1572896 | tf_op jit(solution)/shard_map/ppermute | solution.py:14
  25.6 2.9 fusion.5
  28.5 1.6 collective-permute-start.1
  33.5 0.9 iota_compare_fusion
  34.4 4.5 %fusion.20 = f32[24,64,64]{2,0,1:T(8,128)} fusion(pred[64,64,225]{2,0,1:T(32,128)(4,1)S(1)} %iota_compare_fusion, f32[24,225]{0,1:T(8,128)S(1)} %reshape.290), kind=kOutput, calls=%fused_computation.52 | convolution fusion | flops 265420800 | bytes 1336416 | tf_op jit(solution)/shard_map/hc,qkc->hqk/dot_general | solution.py:116
  38.9 2.3 copy.53
  42.4 0.7 broadcast_compare_fusion
  43.1 53.5 %collective-permute-done.1 = bf16[16,8,4,3072]{3,1,2,0:T(8,128)(2,1)} collective-permute-done((bf16[16,8,4,3072]{3,1,2,0:T(8,128)(2,1)S(1)}, bf16[16,8,4,3072]{3,1,2,0:T(8,128)(2,1)}, u32[]{:S(2)}, u32[]{:S(2)}) %collective-permute-start.1) | collective-permute-done | bytes 3145760 | tf_op jit(solution)/shard_map/ppermute | solution.py:14
  96.6 4.0 %fusion.7 = bf16[16,8,4,3072]{3,1,2,0:T(8,128)(2,1)S(1)} fusion(s32[]{:T(128)S(6)} %select_n.71, bf16[16,8,4,3072]{3,1,2,0:T(8,128)(2,1)S(1)} %fusion.5, bf16[16,8,4,3072]{3,1,2,0:T(8,128)(2,1)} %collective-permute-done.1), kind=kLoop, calls=%fused_computation.17 | loop fusion | flops 6291456 | bytes 9437188 | tf_op jit(solution)/shard_map/concatenate | solution.py:131
  100.6 0.9 copy.76
  101.5 0.9 convert_reduce_fusion
  102.4 2.4 fusion.38
  104.8 1.9 fusion.12
  107.0 4.2 %add_select_fusion = f32[2,24,64,64]{2,3,1,0:T(8,128)S(1)} fusion(f32[24,64,64]{1,2,0:T(8,128)} %copy.53, pred[2,64,64]{1,2,0:T(8,128)(4,1)} %broadcast_compare_fusion, f32[2,64,24,128]{3,2,1,0:T(8,128)} %bitcast.113, f32[128]{0:T(128)S(1)} %get-tuple-element.35, f32[2,64,24]{1,2,0:T(8,128)S(1)} %copy.47, f32[2,64,24]{1,2,0:T(8,128)S(1)} %copy.45, ...), kind=kOutput, calls=%fused_computation.44 | convolution fusion | flops 54067200 | bytes 4383744 | tf_op jit(solution)/shard_map/wqhd,wkhd->whqk/dot_general | solution.py:72
  111.2 1.6 fusion.40
  112.9 3.6 %fusion.19 = bf16[2,64,24,128]{3,1,2,0:T(8,128)(2,1)} fusion(bf16[2,64,24,128]{3,2,1,0:T(8,128)(2,1)} %bitcast.120, f32[2,24,64]{2,1,0:T(8,128)S(1)} %get-tuple-element.38, f32[2,24,64,64]{2,3,1,0:T(8,128)} %copy-done.2), kind=kOutput, calls=%fused_computation.51 | convolution fusion | flops 51317824 | bytes 2371584 | tf_op jit(solution)/shard_map/whqk,wqhd->wkhd/dot_general | solution.py:94
  116.5 3.6 %fusion.18 = bf16[2,64,24,128]{3,1,2,0:T(8,128)(2,1)} fusion(bf16[2,64,24,128]{3,2,1,0:T(8,128)(2,1)} %bitcast.122, f32[2,24,64]{2,1,0:T(8,128)S(1)} %get-tuple-element.38, f32[2,24,64,64]{2,3,1,0:T(8,128)} %copy-done.2), kind=kOutput, calls=%fused_computation.50 | convolution fusion | flops 51317824 | bytes 2371584 | tf_op jit(solution)/shard_map/whqk,wkhd->wqhd/dot_general | solution.py:81
  120.1 2.5 copy.56
  122.6 2.2 stack.22
  124.8 2.5 copy.69
  127.3 2.2 stack.25
  129.5 2.6 multiply_reduce_fusion.2
  132.1 1.4 fusion.29
  133.5 0.7 copy-done.4
  134.2 4.8 %multiply_reduce_fusion = (f32[128]{0:T(128)}, f32[2,64,24]{1,2,0:T(8,128)S(1)}, f32[2,64,24]{1,2,0:T(8,128)S(1)}, f32[2,24,128,64]{2,3,1,0:T(8,128)}) fusion(f32[2,64,24,128]{3,2,1,0:T(8,128)S(1)} %bitcast.111, f32[2,64,24]{1,2,0:T(8,128)S(1)} %copy.50, f32[2,64,24]{1,2,0:T(8,128)S(1)} %copy.48, f32[128]{0:T(128)S(1)} %copy-done.20, ...), kind=kOutput, calls=%fused_computation.36 | convolution fusion | flops 55437184 | bytes 5187072 | tf_op jit(solution)/shard_map/whqk,wqhd->wkhd/dot_general | solution.py:91
  139.0 5.3 %multiply_reduce_fusion.1 = (f32[128]{0:T(128)}, f32[2,64,24]{1,2,0:T(8,128)S(1)}, f32[2,64,24]{1,2,0:T(8,128)S(1)}, f32[2,24,128,64]{2,3,1,0:T(8,128)}) fusion(f32[2,64,24,128]{3,2,1,0:T(8,128)S(1)} %bitcast.115, f32[2,64,24]{1,2,0:T(8,128)S(1)} %copy.47, f32[2,64,24]{1,2,0:T(8,128)S(1)} %copy.45, f32[128]{0:T(128)S(1)} %copy-done.19, ...), kind=kOutput, calls=%fused_computation.37 | convolution fusion | flops 55437184 | bytes 5187072 | tf_op jit(solution)/shard_map/whqk,wkhd->wqhd/dot_general | solution.py:87
  144.9 0.6 broadcast_multiply_fusion.3
  146.2 0.8 copy.63
  147.1 1.4 copy.66
  148.5 1.4 copy.67
  149.9 1.6 multiply_bitcast_fusion
  151.5 0.9 copy.64
  153.2 0.9 copy.60
  154.1 5.1 %multiply_convert_fusion = (bf16[16,8,1,24,128]{4,3,1,2,0:T(8,128)(2,1)}, bf16[16,8,1,24,128]{4,3,1,2,0:T(8,128)(2,1)}) fusion(f32[16,8,1,24,128]{4,3,1,2,0:T(8,128)S(1)} %bitcast.108, f32[16,8,24]{2,1,0:T(8,128)S(1)} %bitcast.129, f32[16,8,24]{2,1,0:T(8,128)S(1)} %get-tuple-element.46, f32[16,8,24]{2,1,0:T(8,128)S(1)} %bitcast.128, ...), kind=kLoop, calls=%fused_computation.38 | loop fusion | flops 7077888 | bytes 6390784 | tf_op jit(solution)/shard_map/convert.8
  159.2 1.5 stack.24
  161.3 1.0 copy-done.5
  162.5 1.5 copy-done
  165.4 21.3 %collective-permute-done.2 = bf16[8,8,4,3072]{3,1,0,2:T(8,128)(2,1)} collective-permute-done((bf16[8,8,4,3072]{3,1,0,2:T(8,128)(2,1)S(1)}, bf16[8,8,4,3072]{3,1,0,2:T(8,128)(2,1)}, u32[]{:S(2)}, u32[]{:S(2)}) %collective-permute-start.2) | collective-permute-done | bytes 1572896 | tf_op jit(solution)/shard_map/ppermute | solution.py:14
  186.7 2.6 fusion.3
  189.3 1.6 collective-permute-start.3
  192.1 2.8 convolution_bitcast_fusion
  195.0 95.8 %all-reduce = (f32[2,128]{1,0:T(2,128)}, f32[24,15,15]{2,1,0:T(8,128)S(1)}) all-reduce(f32[2,128]{1,0:T(2,128)S(1)} %pad_maximum_fusion.1, f32[24,15,15]{2,1,0:T(8,128)S(1)} %reshape.285), channel_id=1, replica_groups=mesh['row'=16,'col'=2] {'row','col'}, use_global_device_ids=true, to_apply=%region_13.14 | all-reduce | flops 5656 | bytes 45248 | tf_op jit(solution)/shard_map/psum | solution.py:170
  290.9 0.8 copy.72
  291.7 4.0 %fusion.6 = bf16[16,8,4,3072]{3,1,0,2:T(8,128)(2,1)S(1)} fusion(s32[]{:T(128)S(6)} %select_n.80, bf16[16,8,4,3072]{3,1,0,2:T(8,128)(2,1)} %collective-permute-done.3, bf16[16,8,4,3072]{3,1,0,2:T(8,128)(2,1)S(1)} %fusion.3), kind=kLoop, calls=%fused_computation.16 | loop fusion | flops 6291456 | bytes 9437188 | tf_op jit(solution)/shard_map/concatenate | solution.py:165
  295.8 0.9 slice_bitcast_fusion
  296.8 1.6 copy.71
  (72 shorter events, 5.5 us)
Async XLA Ops:
  0.6 7.1 %copy-start.16 = (s32[2]{0:T(128)S(1)}, s32[2]{0:T(128)}, u32[]{:S(2)}) copy-start(s32[2]{0:T(128)} %param.10) | copy-start | bytes 28
  2.2 23.4 %collective-permute-start = (bf16[8,8,4,3072]{3,1,2,0:T(8,128)(2,1)S(1)}, bf16[8,8,4,3072]{3,1,2,0:T(8,128)(2,1)}, u32[]{:S(2)}, u32[]{:S(2)}) collective-permute-start(bf16[8,8,4,3072]{3,1,2,0:T(8,128)(2,1)S(1)} %pad_maximum_fusion), channel_id=1, source_target_pairs={{0,30},{2,0},{4,2},{6,4},{8,6},{10,8},{12,10},{14,12},{16,14},{18,... | collective-permute-start | bytes 4718600 | tf_op jit(solution)/shard_map/ppermute | solution.py:14
  10.2 22.3 %copy-start.14 = (s32[256,16]{0,1:T(8,128)S(1)}, s32[256,16]{0,1:T(8,128)}, u32[]{:S(2)}) copy-start(s32[256,16]{0,1:T(8,128)} %param.11) | copy-start | bytes 49156
  10.2 22.5 %copy-start.13 = (f32[24,15,15]{0,2,1:T(8,128)S(1)}, f32[24,15,15]{0,2,1:T(8,128)}, u32[]{:S(2)}) copy-start(f32[24,15,15]{0,2,1:T(8,128)} %param.9) | copy-start | bytes 64804
  28.5 68.1 %collective-permute-start.1 = (bf16[16,8,4,3072]{3,1,2,0:T(8,128)(2,1)S(1)}, bf16[16,8,4,3072]{3,1,2,0:T(8,128)(2,1)}, u32[]{:S(2)}, u32[]{:S(2)}) collective-permute-start(bf16[16,8,4,3072]{3,1,2,0:T(8,128)(2,1)S(1)} %fusion.5), channel_id=1, source_target_pairs={{0,1},{1,0},{2,3},{3,2},{4,5},{5,4},{6,7},{7,6},{8,9},{9,8},{10,11... | collective-permute-start | bytes 9437192 | tf_op jit(solution)/shard_map/ppermute | solution.py:14
  32.9 0.6 copy-start.11
  38.9 2.9 copy-start.15
  111.2 1.7 copy-start.2
  129.5 2.6 copy-start.1
  132.1 1.4 copy-start.3
  132.1 2.2 copy-start.4
  132.1 2.1 copy-start.20
  134.2 4.8 %copy-start.19 = (f32[128]{0:T(128)S(1)}, f32[128]{0:T(128)}, u32[]{:S(2)}) copy-start(f32[128]{0:T(128)} %get-tuple-element.33) | copy-start | bytes 1540
  151.5 1.4 copy-start.8
  153.2 0.9 copy-start.9
  153.2 0.9 copy-start.10
  159.2 1.6 copy-start.7
  159.2 1.9 copy-start.6
  161.2 1.1 copy-start.5
  162.4 1.7 copy-start
  164.1 22.6 %collective-permute-start.2 = (bf16[8,8,4,3072]{3,1,0,2:T(8,128)(2,1)S(1)}, bf16[8,8,4,3072]{3,1,0,2:T(8,128)(2,1)}, u32[]{:S(2)}, u32[]{:S(2)}) collective-permute-start(bf16[8,8,4,3072]{3,1,0,2:T(8,128)(2,1)S(1)} %slice.56), channel_id=1, source_target_pairs={{0,2},{2,4},{4,6},{6,8},{8,10},{10,12},{12,14},{14,16},{16,18},{18... | collective-permute-start | bytes 4718600 | tf_op jit(solution)/shard_map/ppermute | solution.py:14
  165.4 26.7 %copy-start.12 = (s32[64,64]{0,1:T(8,128)S(1)}, s32[64,64]{0,1:T(8,128)}, u32[]{:S(2)}) copy-start(s32[64,64]{0,1:T(8,128)} %copy-done.11) | copy-start | bytes 49156
  189.3 5.7 %copy-start.17 = (f32[128]{0:T(128)S(1)}, f32[128]{0:T(128)}, u32[]{:S(2)}) copy-start(f32[128]{0:T(128)} %get-tuple-element.14) | copy-start | bytes 1540
  189.3 5.7 %copy-start.18 = (f32[128]{0:T(128)S(1)}, f32[128]{0:T(128)}, u32[]{:S(2)}) copy-start(f32[128]{0:T(128)} %get-tuple-element.12) | copy-start | bytes 1540
  189.3 102.4 %collective-permute-start.3 = (bf16[16,8,4,3072]{3,1,0,2:T(8,128)(2,1)S(1)}, bf16[16,8,4,3072]{3,1,0,2:T(8,128)(2,1)}, u32[]{:S(2)}, u32[]{:S(2)}) collective-permute-start(bf16[16,8,4,3072]{3,1,0,2:T(8,128)(2,1)S(1)} %fusion.3), channel_id=1, source_target_pairs={{0,1},{1,0},{2,3},{3,2},{4,5},{5,4},{6,7},{7,6},{8,9},{9,8},{10,11... | collective-permute-start | bytes 9437192 | tf_op jit(solution)/shard_map/ppermute | solution.py:14
where the time goes:
time: 299 us; the launch traced here: 298 us
  blocking collectives  95.8 us (32%)
  waiting for transfers between devices  90.2 us (30%)
  other arithmetic  34.4 us (12%)
  matrix products  31.4 us (11%)
  local copies, waits for them, and re-layouts  29.4 us (10%)
  starting transfers between devices  8.67 us (3%)
  between operations  8.46 us (3%)
    psum x1, blocking collectives, local(): lax.psum((jnp.stack([dgain_q, dgain_k]), table_local), ('row', 'col'))  95.8 us
    ppermute x4, waiting for transfers between devices, shifted(): return lax.ppermute(value, axis, pairs)  90.2 us
    ppermute x4, starting transfers between devices, shifted(): return lax.ppermute(value, axis, pairs)  8.67 us
    unnamed x48, local copies, waits for them, and re-layouts  7.83 us
    another operation x5, local copies, waits for them, and re-layouts, local(): jnp.stack([output, d_query, d_key, d_value], axis=2)  6.26 us
  transfers between devices with their start and end apart: 4, of which 3 were waited for; matrix products, arithmetic and copies ran while one was open for 5% of the time, Pallas kernels for 0%

commit v1 on v0

--- a/solution.py
+++ b/solution.py
@@ -167,7 +167,7 @@
     attention = results[:, :, 0]
     d_qkv = results[:, :, 1:]
     table_local = jnp.einsum("hqk,qkc->hc", d_bias, one_hot, precision=lax.Precision.HIGHEST)
-    totals = lax.psum((jnp.stack([dgain_q, dgain_k]), table_local), ("row", "col"))
+    totals = lax.psum(lax.psum((jnp.stack([dgain_q, dgain_k]), table_local), "col"), "row")
     return (attention, d_qkv, totals[0], totals[1].reshape(head_count, span_count, span_count))
 
 

time: 299 us -> 329 us (1.10)
  blocking collectives: 95.8 us -> 125 us
    psum x1 -> x2, blocking collectives: 95.8 us -> 125 us  [the longest x1 63.2 us: local(): lax.psum(lax.psum((jnp.stack([dgain_q, dgain_k]), table_local), 'col'), '...]
  transfers between devices with their start and end apart: 4 -> 4, of which waited for: 3 -> 3; matrix products, arithmetic and copies ran while one was open for 5% -> 4% of each run, Pallas kernels for 0% -> 0%
where the time goes in v1:
time: 329 us; the launch traced here: 328 us
  blocking collectives  125 us (38%)
  waiting for transfers between devices  90.2 us (27%)
  other arithmetic  34.4 us (10%)
  matrix products  31.4 us (10%)
  local copies, waits for them, and re-layouts  29.4 us (9%)
  starting transfers between devices  8.67 us (3%)
  between operations  8.46 us (3%)
    ppermute x4, waiting for transfers between devices, shifted(): return lax.ppermute(value, axis, pairs)  90.2 us
    psum x1, blocking collectives, local(): lax.psum(lax.psum((jnp.stack([dgain_q, dgain_k]), table_local), 'col'), '...  63.2 us
    psum x1, blocking collectives, local(): lax.psum((jnp.stack([dgain_q, dgain_k]), table_local), 'col')  61.9 us
    ppermute x4, starting transfers between devices, shifted(): return lax.ppermute(value, axis, pairs)  8.67 us
    unnamed x48, local copies, waits for them, and re-layouts  7.83 us
  transfers between devices with their start and end apart: 4, of which 3 were waited for; matrix products, arithmetic and copies ran while one was open for 4% of the time, Pallas kernels for 0%

profile of v1, /device:TPU:0, one launch (start us, length us, event | category | flops | bytes accessed | tf_op | source)
XLA Modules:
  0.0 327.6 jit_solution(12330337860898563708)
XLA Ops:
  0.6 1.5 pad_maximum_fusion
  2.2 5.5 %collective-permute-start = (bf16[8,8,4,3072]{3,1,2,0:T(8,128)(2,1)S(1)}, bf16[8,8,4,3072]{3,1,2,0:T(8,128)(2,1)}, u32[]{:S(2)}, u32[]{:S(2)}) collective-permute-start(bf16[8,8,4,3072]{3,1,2,0:T(8,128)(2,1)S(1)} %pad_maximum_fusion), channel_id=1, source_target_pairs={{0,30},{2,0},{4,2},{6,4},{8,6},{10,8},{12,10},{14,12},{16,14},{18,... | collective-permute-start | bytes 4718600 | tf_op jit(solution)/shard_map/ppermute | solution.py:14
  10.2 15.4 %collective-permute-done = bf16[8,8,4,3072]{3,1,2,0:T(8,128)(2,1)} collective-permute-done((bf16[8,8,4,3072]{3,1,2,0:T(8,128)(2,1)S(1)}, bf16[8,8,4,3072]{3,1,2,0:T(8,128)(2,1)}, u32[]{:S(2)}, u32[]{:S(2)}) %collective-permute-start) | collective-permute-done | bytes 1572896 | tf_op jit(solution)/shard_map/ppermute | solution.py:14
  25.6 2.9 fusion.5
  28.5 1.6 collective-permute-start.1
  33.5 0.9 iota_compare_fusion
  34.4 4.5 %fusion.20 = f32[24,64,64]{2,0,1:T(8,128)} fusion(pred[64,64,225]{2,0,1:T(32,128)(4,1)S(1)} %iota_compare_fusion, f32[24,225]{0,1:T(8,128)S(1)} %reshape.290), kind=kOutput, calls=%fused_computation.52 | convolution fusion | flops 265420800 | bytes 1336416 | tf_op jit(solution)/shard_map/hc,qkc->hqk/dot_general | solution.py:116
  38.9 2.3 copy.53
  42.4 0.7 broadcast_compare_fusion
  43.1 53.5 %collective-permute-done.1 = bf16[16,8,4,3072]{3,1,2,0:T(8,128)(2,1)} collective-permute-done((bf16[16,8,4,3072]{3,1,2,0:T(8,128)(2,1)S(1)}, bf16[16,8,4,3072]{3,1,2,0:T(8,128)(2,1)}, u32[]{:S(2)}, u32[]{:S(2)}) %collective-permute-start.1) | collective-permute-done | bytes 3145760 | tf_op jit(solution)/shard_map/ppermute | solution.py:14
  96.6 4.0 %fusion.7 = bf16[16,8,4,3072]{3,1,2,0:T(8,128)(2,1)S(1)} fusion(s32[]{:T(128)S(6)} %select_n.71, bf16[16,8,4,3072]{3,1,2,0:T(8,128)(2,1)S(1)} %fusion.5, bf16[16,8,4,3072]{3,1,2,0:T(8,128)(2,1)} %collective-permute-done.1), kind=kLoop, calls=%fused_computation.17 | loop fusion | flops 6291456 | bytes 9437188 | tf_op jit(solution)/shard_map/concatenate | solution.py:131
  100.6 0.9 copy.76
  101.5 0.9 convert_reduce_fusion
  102.4 2.4 fusion.38
  104.8 1.9 fusion.12
  107.0 4.2 %add_select_fusion = f32[2,24,64,64]{2,3,1,0:T(8,128)S(1)} fusion(f32[24,64,64]{1,2,0:T(8,128)} %copy.53, pred[2,64,64]{1,2,0:T(8,128)(4,1)} %broadcast_compare_fusion, f32[2,64,24,128]{3,2,1,0:T(8,128)} %bitcast.113, f32[128]{0:T(128)S(1)} %get-tuple-element.37, f32[2,64,24]{1,2,0:T(8,128)S(1)} %copy.47, f32[2,64,24]{1,2,0:T(8,128)S(1)} %copy.45, ...), kind=kOutput, calls=%fused_computation.44 | convolution fusion | flops 54067200 | bytes 4383744 | tf_op jit(solution)/shard_map/wqhd,wkhd->whqk/dot_general | solution.py:72
  111.2 1.6 fusion.40
  112.9 3.6 %fusion.19 = bf16[2,64,24,128]{3,1,2,0:T(8,128)(2,1)} fusion(bf16[2,64,24,128]{3,2,1,0:T(8,128)(2,1)} %bitcast.120, f32[2,24,64]{2,1,0:T(8,128)S(1)} %get-tuple-element.40, f32[2,24,64,64]{2,3,1,0:T(8,128)} %copy-done.2), kind=kOutput, calls=%fused_computation.51 | convolution fusion | flops 51317824 | bytes 2371584 | tf_op jit(solution)/shard_map/whqk,wqhd->wkhd/dot_general | solution.py:94
  116.5 3.6 %fusion.18 = bf16[2,64,24,128]{3,1,2,0:T(8,128)(2,1)} fusion(bf16[2,64,24,128]{3,2,1,0:T(8,128)(2,1)} %bitcast.122, f32[2,24,64]{2,1,0:T(8,128)S(1)} %get-tuple-element.40, f32[2,24,64,64]{2,3,1,0:T(8,128)} %copy-done.2), kind=kOutput, calls=%fused_computation.50 | convolution fusion | flops 51317824 | bytes 2371584 | tf_op jit(solution)/shard_map/whqk,wkhd->wqhd/dot_general | solution.py:81
  120.1 2.5 copy.56
  122.6 2.2 stack.22
  124.8 2.5 copy.69
  127.3 2.2 stack.25
  129.5 2.6 multiply_reduce_fusion.2
  132.1 1.4 fusion.29
  133.5 0.7 copy-done.4
  134.2 4.8 %multiply_reduce_fusion = (f32[128]{0:T(128)}, f32[2,64,24]{1,2,0:T(8,128)S(1)}, f32[2,64,24]{1,2,0:T(8,128)S(1)}, f32[2,24,128,64]{2,3,1,0:T(8,128)}) fusion(f32[2,64,24,128]{3,2,1,0:T(8,128)S(1)} %bitcast.111, f32[2,64,24]{1,2,0:T(8,128)S(1)} %copy.50, f32[2,64,24]{1,2,0:T(8,128)S(1)} %copy.48, f32[128]{0:T(128)S(1)} %copy-done.20, ...), kind=kOutput, calls=%fused_computation.36 | convolution fusion | flops 55437184 | bytes 5187072 | tf_op jit(solution)/shard_map/whqk,wqhd->wkhd/dot_general | solution.py:91
  139.0 5.3 %multiply_reduce_fusion.1 = (f32[128]{0:T(128)}, f32[2,64,24]{1,2,0:T(8,128)S(1)}, f32[2,64,24]{1,2,0:T(8,128)S(1)}, f32[2,24,128,64]{2,3,1,0:T(8,128)}) fusion(f32[2,64,24,128]{3,2,1,0:T(8,128)S(1)} %bitcast.115, f32[2,64,24]{1,2,0:T(8,128)S(1)} %copy.47, f32[2,64,24]{1,2,0:T(8,128)S(1)} %copy.45, f32[128]{0:T(128)S(1)} %copy-done.19, ...), kind=kOutput, calls=%fused_computation.37 | convolution fusion | flops 55437184 | bytes 5187072 | tf_op jit(solution)/shard_map/whqk,wkhd->wqhd/dot_general | solution.py:87
  146.2 0.8 copy.63
  147.1 1.4 copy.66
  148.5 1.4 copy.67
  149.9 1.6 multiply_bitcast_fusion
  151.5 0.9 copy.64
  153.2 0.9 copy.60
  154.1 5.1 %multiply_convert_fusion = (bf16[16,8,1,24,128]{4,3,1,2,0:T(8,128)(2,1)}, bf16[16,8,1,24,128]{4,3,1,2,0:T(8,128)(2,1)}) fusion(f32[16,8,1,24,128]{4,3,1,2,0:T(8,128)S(1)} %bitcast.108, f32[16,8,24]{2,1,0:T(8,128)S(1)} %bitcast.129, f32[16,8,24]{2,1,0:T(8,128)S(1)} %get-tuple-element.48, f32[16,8,24]{2,1,0:T(8,128)S(1)} %bitcast.128, ...), kind=kLoop, calls=%fused_computation.38 | loop fusion | flops 7077888 | bytes 6390784 | tf_op jit(solution)/shard_map/convert.8
  159.2 1.5 stack.24
  161.3 1.0 copy-done.5
  162.5 1.5 copy-done
  165.4 21.3 %collective-permute-done.2 = bf16[8,8,4,3072]{3,1,0,2:T(8,128)(2,1)} collective-permute-done((bf16[8,8,4,3072]{3,1,0,2:T(8,128)(2,1)S(1)}, bf16[8,8,4,3072]{3,1,0,2:T(8,128)(2,1)}, u32[]{:S(2)}, u32[]{:S(2)}) %collective-permute-start.2) | collective-permute-done | bytes 1572896 | tf_op jit(solution)/shard_map/ppermute | solution.py:14
  186.7 2.6 fusion.3
  189.3 1.6 collective-permute-start.3
  192.1 2.8 convolution_bitcast_fusion
  194.9 61.9 %all-reduce.1 = (f32[2,128]{1,0:T(2,128)S(1)}, f32[24,225]{1,0:T(8,128)S(1)}) all-reduce(f32[2,128]{1,0:T(2,128)S(1)} %pad_maximum_fusion.1, f32[24,225]{1,0:T(8,128)S(1)} %convolution_bitcast_fusion), channel_id=1, replica_groups=mesh['row'=16,'col'=2] {'col'}, use_global_device_ids=true, to_apply=%region_13.14 | all-reduce | flops 5656 | bytes 45248 | tf_op jit(solution)/shard_map/psum | solution.py:170
  256.9 63.2 %all-reduce = (f32[2,128]{1,0:T(2,128)}, f32[24,15,15]{2,1,0:T(8,128)S(1)}) all-reduce(f32[2,128]{1,0:T(2,128)S(1)} %get-tuple-element.24, f32[24,15,15]{2,1,0:T(8,128)S(1)} %reshape.285), channel_id=1, replica_groups=mesh['row'=16,'col'=2] {'row'}, use_global_device_ids=true, to_apply=%region_14.15 | all-reduce | flops 5656 | bytes 45248 | tf_op jit(solution)/shard_map/psum | solution.py:170
  320.1 0.8 copy.72
  321.0 4.0 %fusion.6 = bf16[16,8,4,3072]{3,1,0,2:T(8,128)(2,1)S(1)} fusion(s32[]{:T(128)S(6)} %select_n.80, bf16[16,8,4,3072]{3,1,0,2:T(8,128)(2,1)} %collective-permute-done.3, bf16[16,8,4,3072]{3,1,0,2:T(8,128)(2,1)S(1)} %fusion.3), kind=kLoop, calls=%fused_computation.16 | loop fusion | flops 6291456 | bytes 9437188 | tf_op jit(solution)/shard_map/concatenate | solution.py:165
  325.0 0.9 slice_bitcast_fusion
  326.1 1.6 copy.71
  (73 shorter events, 6.1 us)
Async XLA Ops:
  0.6 7.1 %copy-start.16 = (s32[2]{0:T(128)S(1)}, s32[2]{0:T(128)}, u32[]{:S(2)}) copy-start(s32[2]{0:T(128)} %param.10) | copy-start | bytes 28
  2.2 23.4 %collective-permute-start = (bf16[8,8,4,3072]{3,1,2,0:T(8,128)(2,1)S(1)}, bf16[8,8,4,3072]{3,1,2,0:T(8,128)(2,1)}, u32[]{:S(2)}, u32[]{:S(2)}) collective-permute-start(bf16[8,8,4,3072]{3,1,2,0:T(8,128)(2,1)S(1)} %pad_maximum_fusion), channel_id=1, source_target_pairs={{0,30},{2,0},{4,2},{6,4},{8,6},{10,8},{12,10},{14,12},{16,14},{18,... | collective-permute-start | bytes 4718600 | tf_op jit(solution)/shard_map/ppermute | solution.py:14
  10.2 22.3 %copy-start.14 = (s32[256,16]{0,1:T(8,128)S(1)}, s32[256,16]{0,1:T(8,128)}, u32[]{:S(2)}) copy-start(s32[256,16]{0,1:T(8,128)} %param.11) | copy-start | bytes 49156
  10.2 22.5 %copy-start.13 = (f32[24,15,15]{0,2,1:T(8,128)S(1)}, f32[24,15,15]{0,2,1:T(8,128)}, u32[]{:S(2)}) copy-start(f32[24,15,15]{0,2,1:T(8,128)} %param.9) | copy-start | bytes 64804
  28.5 68.1 %collective-permute-start.1 = (bf16[16,8,4,3072]{3,1,2,0:T(8,128)(2,1)S(1)}, bf16[16,8,4,3072]{3,1,2,0:T(8,128)(2,1)}, u32[]{:S(2)}, u32[]{:S(2)}) collective-permute-start(bf16[16,8,4,3072]{3,1,2,0:T(8,128)(2,1)S(1)} %fusion.5), channel_id=1, source_target_pairs={{0,1},{1,0},{2,3},{3,2},{4,5},{5,4},{6,7},{7,6},{8,9},{9,8},{10,11... | collective-permute-start | bytes 9437192 | tf_op jit(solution)/shard_map/ppermute | solution.py:14
  32.9 0.6 copy-start.11
  38.9 2.9 copy-start.15
  111.2 1.7 copy-start.2
  129.5 2.6 copy-start.1
  132.1 1.4 copy-start.3
  132.1 2.2 copy-start.4
  132.1 2.1 copy-start.20
  134.2 4.8 %copy-start.19 = (f32[128]{0:T(128)S(1)}, f32[128]{0:T(128)}, u32[]{:S(2)}) copy-start(f32[128]{0:T(128)} %get-tuple-element.35) | copy-start | bytes 1540
  151.5 1.4 copy-start.8
  153.2 0.9 copy-start.9
  153.2 0.9 copy-start.10
  159.2 1.6 copy-start.7
  159.2 1.9 copy-start.6
  161.2 1.1 copy-start.5
  162.4 1.7 copy-start
  164.1 22.6 %collective-permute-start.2 = (bf16[8,8,4,3072]{3,1,0,2:T(8,128)(2,1)S(1)}, bf16[8,8,4,3072]{3,1,0,2:T(8,128)(2,1)}, u32[]{:S(2)}, u32[]{:S(2)}) collective-permute-start(bf16[8,8,4,3072]{3,1,0,2:T(8,128)(2,1)S(1)} %slice.56), channel_id=1, source_target_pairs={{0,2},{2,4},{4,6},{6,8},{8,10},{10,12},{12,14},{14,16},{16,18},{18... | collective-permute-start | bytes 4718600 | tf_op jit(solution)/shard_map/ppermute | solution.py:14
  165.4 26.7 %copy-start.17 = (f32[128]{0:T(128)S(1)}, f32[128]{0:T(128)}, u32[]{:S(2)}) copy-start(f32[128]{0:T(128)} %get-tuple-element.14) | copy-start | bytes 1540
  165.4 26.7 %copy-start.18 = (f32[128]{0:T(128)S(1)}, f32[128]{0:T(128)}, u32[]{:S(2)}) copy-start(f32[128]{0:T(128)} %get-tuple-element.12) | copy-start | bytes 1540
  165.4 26.7 %copy-start.12 = (s32[64,64]{0,1:T(8,128)S(1)}, s32[64,64]{0,1:T(8,128)}, u32[]{:S(2)}) copy-start(s32[64,64]{0,1:T(8,128)} %copy-done.11) | copy-start | bytes 49156
  189.3 131.7 %collective-permute-start.3 = (bf16[16,8,4,3072]{3,1,0,2:T(8,128)(2,1)S(1)}, bf16[16,8,4,3072]{3,1,0,2:T(8,128)(2,1)}, u32[]{:S(2)}, u32[]{:S(2)}) collective-permute-start(bf16[16,8,4,3072]{3,1,0,2:T(8,128)(2,1)S(1)} %fusion.3), channel_id=1, source_target_pairs={{0,1},{1,0},{2,3},{3,2},{4,5},{5,4},{6,7},{7,6},{8,9},{9,8},{10,11... | collective-permute-start | bytes 9437192 | tf_op jit(solution)/shard_map/ppermute | solution.py:14
